TPU v7x, 512 devices: a whole 4x4x16 slice. The times are simulated.
512 devices in a mesh: slot: 16 (over z_lo, x), row: 32 (over y, z_hi, core).
Axes of the slice: x: 4, y: 4, z: 16 (z_hi: 4, z_lo: 4; z = z_hi * 4 + z_lo), core: 2. Of those that a mesh axis runs over, the one named last changes fastest.
Arguments:
- drift: bfloat16 [2048, 2048], P(('slot', 'row')), may hold values from -1 to 1, as said below
- ctrl_blocks: bfloat16 [16, 128, 128], replicated, may hold values from -0.125 to 0.125
- blk_pos: int32 [16, 2], replicated, may hold values from 0 to 15
- amps: float32 [16, 16], P('slot'), may hold values from -4 to 4
- init_states: float32 [2, 512, 2048], P(None, 'row'), may hold values from -6 to 6
- targets: float32 [2, 512, 2048], P(None, 'row'), may hold values from -50 to 50
Outputs:
- states: float32 [16, 2, 512, 2048], P('slot', None, 'row')
- grads: float32 [16, 16], P('slot')
Inputs may be any that keep to these rules, and one draw needn't show every extreme that they name: drift is symmetric.
All inputs are finite; a program needn't handle non-finite values.
Results may differ from a plain program's by a relative error of at most 0.038.
Values may be sent and summed in bfloat16 or wider, within the bound.
No kernel may reach another device: no remote copies, remote signals or barrier semaphores. Data moves between devices by JAX's collectives and lax.ppermute only.
A program may use at most 64 MiB of HBM per device.

v0:
```python
import jax
import jax.numpy as jnp
from jax import lax
from jax.sharding import PartitionSpec as P

TAYLOR = 4


def passed_along(value, axis, steps):
    count = lax.axis_size(axis)
    initial, last = (max(0, -steps), min(count, count - steps))
    return lax.ppermute(value, axis, [(source, source + steps) for source in range(initial, last)])


def apply_hamiltonian(
    rounded, drift_full, ctrl_blocks, row_pick, col_pick, row_hot, col_hot, amps_row
):
    halves, columns, extent = rounded.shape
    block_size = ctrl_blocks.shape[1]
    flat_rows = rounded.reshape(halves * columns, extent)
    drift_part = jnp.dot(flat_rows, drift_full, preferred_element_type=jnp.float32)
    tile_rows = flat_rows.reshape(halves * columns, extent // block_size, block_size)
    from_col = jnp.take(tile_rows, col_pick, axis=1)
    from_row = jnp.take(tile_rows, row_pick, axis=1)
    upper_part = (
        jnp.einsum("mkb,kab->mka", from_col, ctrl_blocks, preferred_element_type=jnp.float32)
        * amps_row[None, :, None]
    )
    lower_part = (
        jnp.einsum("mka,kab->mkb", from_row, ctrl_blocks, preferred_element_type=jnp.float32)
        * amps_row[None, :, None]
    )
    placed = jnp.einsum("mka,kn->mna", upper_part, row_hot, precision=lax.Precision.HIGHEST)
    placed = placed + jnp.einsum(
        "mkb,kn->mnb", lower_part, col_hot, precision=lax.Precision.HIGHEST
    )
    summed = drift_part + placed.reshape(halves * columns, extent)
    return summed.reshape(halves, columns, extent)


def propagate(state, forward, apply_fn):
    summed = state
    series_term = state
    for degree in range(1, TAYLOR + 1):
        applied = apply_fn(series_term.astype(jnp.bfloat16))
        if forward:
            turned = jnp.stack([applied[1], -applied[0]])
        else:
            turned = jnp.stack([-applied[1], applied[0]])
        series_term = turned * (1.0 / degree)
        summed = summed + series_term
    return summed


def control_grads(state, adjoint, ctrl_blocks, row_pick, col_pick, scale):
    halves, columns, extent = state.shape
    block_size = ctrl_blocks.shape[1]
    shape_tiles = (halves * columns, extent // block_size, block_size)
    source = jnp.stack([state[1].astype(jnp.bfloat16), -state[0].astype(jnp.bfloat16)]).reshape(
        shape_tiles
    )
    weights = adjoint.astype(jnp.bfloat16).reshape(shape_tiles)
    upper_part = jnp.einsum(
        "mkb,kab->mka",
        jnp.take(source, col_pick, axis=1),
        ctrl_blocks,
        preferred_element_type=jnp.float32,
    )
    lower_part = jnp.einsum(
        "mka,kab->mkb",
        jnp.take(source, row_pick, axis=1),
        ctrl_blocks,
        preferred_element_type=jnp.float32,
    )
    inner_sum = jnp.sum(
        jnp.take(weights, row_pick, axis=1).astype(jnp.float32) * upper_part, axis=(0, 2)
    )
    inner_sum = inner_sum + jnp.sum(
        jnp.take(weights, col_pick, axis=1).astype(jnp.float32) * lower_part, axis=(0, 2)
    )
    return inner_sum * scale


def blank(values):
    return jnp.zeros_like(values)


def shards(drift, ctrl_blocks, blk_pos, amps, init_states, targets):
    drift_full = lax.all_gather(drift, ("slot", "row"), axis=0, tiled=True)
    block_count = drift_full.shape[0] // ctrl_blocks.shape[1]
    row_pick = blk_pos[:, 0]
    col_pick = blk_pos[:, 1]
    positions = lax.broadcasted_iota(jnp.int32, (ctrl_blocks.shape[0], block_count), 1)
    row_hot = (positions == row_pick[:, None]).astype(jnp.float32)
    col_hot = (positions == col_pick[:, None]).astype(jnp.float32)
    amps_row = amps[0]

    def apply_fn(rounded):
        return apply_hamiltonian(
            rounded, drift_full, ctrl_blocks, row_pick, col_pick, row_hot, col_hot, amps_row
        )

    def forward_map(values):
        return propagate(values, True, apply_fn)

    def adjoint_map(values):
        return propagate(values, False, apply_fn)

    slot_index = lax.axis_index("slot")
    slot_count = lax.axis_size("slot")
    last_slot = slot_count - 1
    columns = init_states.shape[1]
    extent = init_states.shape[2]
    piece_count = 1
    width = columns // piece_count

    def split_cols(values):
        return values.reshape(2, piece_count, width, extent).transpose(1, 0, 2, 3)

    def join_cols(pieces):
        return pieces.transpose(1, 0, 2, 3).reshape(2, columns, extent)

    init_pieces = split_cols(init_states)
    target_pieces = split_cols(targets)
    tick_count = slot_count + piece_count - 1
    empty_all = jnp.zeros_like(init_pieces)
    empty_one = jnp.zeros_like(init_pieces[0])

    def forward_update(step, stored, arrived):
        order = step - slot_index
        active = (order >= 0) & (order < piece_count)
        place = jnp.clip(order, 0, piece_count - 1)
        start_piece = lax.dynamic_index_in_dim(init_pieces, place, 0, keepdims=False)
        source = jnp.where(slot_index == 0, start_piece, arrived)
        result = lax.cond(active, forward_map, blank, source)
        updated = lax.dynamic_update_index_in_dim(stored, result, place, 0)
        stored = jnp.where(active, updated, stored)
        return (stored, result)

    def adjoint_update(step, stored, returned):
        order = step - (last_slot - slot_index)
        active = (order >= 0) & (order < piece_count)
        place = jnp.clip(order, 0, piece_count - 1)
        target_piece = lax.dynamic_index_in_dim(target_pieces, place, 0, keepdims=False)
        own = jnp.where(slot_index == last_slot, target_piece, returned)
        updated = lax.dynamic_update_index_in_dim(stored, own, place, 0)
        stored = jnp.where(active, updated, stored)
        outgoing = lax.cond(active & (slot_index > 0), adjoint_map, blank, own)
        return (stored, outgoing)

    def joint_tick(step, carry):
        fwd_stored, fwd_out, adj_stored, adj_out = carry
        arrived = passed_along(fwd_out.astype(jnp.bfloat16), "slot", 1).astype(fwd_out.dtype)
        returned = passed_along(adj_out.astype(jnp.bfloat16), "slot", -1).astype(adj_out.dtype)
        fwd_stored, fwd_out = forward_update(step, fwd_stored, arrived)
        adj_stored, adj_out = adjoint_update(step, adj_stored, returned)
        return (fwd_stored, fwd_out, adj_stored, adj_out)

    fwd_stored, _, adj_stored, _ = lax.fori_loop(
        0, tick_count, joint_tick, (empty_all, empty_one, empty_all, empty_one)
    )
    fwd_state = join_cols(fwd_stored)
    adj_mine = join_cols(adj_stored)
    scale = 1.0 / (columns * lax.axis_size("row"))
    partial_grads = control_grads(fwd_state, adj_mine, ctrl_blocks, row_pick, col_pick, scale)
    grads = lax.psum(partial_grads[None, :], "row")
    return (fwd_state[None], grads)


def solution(mesh):
    in_specs = (
        P(("slot", "row"), None),
        P(),
        P(),
        P("slot", None),
        P(None, "row", None),
        P(None, "row", None),
    )
    out_specs = (P("slot", None, "row", None), P("slot", None))
    return jax.shard_map(shards, mesh=mesh, in_specs=in_specs, out_specs=out_specs, check_vma=False)
```

profile of v0, /device:TPU:103, one launch (start us, length us, event | category | flops | bytes accessed | tf_op | source)
XLA Modules:
  0.0 1654.7 jit_solution(1172429229301434716)
XLA Ops:
  7.9 1.3 compare_and_fusion.5
  11.2 817.7 %all-gather.3.cloned.1.call-done = bf16[512,4,2048]{2,1,0:T(4,128)(2,1)} async-done(((bf16[1,4,2048]{2,1,0:T(4,128)(2,1)}), bf16[512,4,2048]{2,1,0:T(4,128)(2,1)}) %all-gather.3.cloned.1.call-update) | async-done | bytes 8388624 | tf_op jit(solution)/shard_map/all_gather | solution.py:89
  828.9 12.5 reshape.382
  842.2 692.2 %while.23 = (s32[]{:T(128)}, f32[1,2,16,2048]{3,2,1,0:T(8,128)S(1)}, f32[2,16,2048]{2,1,0:T(8,128)}, bf16[1,2,16,2048]{3,2,1,0:T(8,128)(2,1)S(1)}, bf16[2,16,204...) while((s32[]{:T(128)}, ...), condition=%wide.region_5.7_spmd.clone.clone.clone, body=%wide.region_0.6_spmd.clone.clone.clone.sunk | while | flops 2623804928 | bytes 120887232 | solution.py:159
  842.2 1.0 convert_element_type.216
  843.2 1.3 collective-permute-start
  844.5 4.0 collective-permute-start.1
  848.6 2.2 collective-permute-done.1
  851.7 32.8 %conditional.11 = (bf16[2,16,2048]{2,1,0:T(8,128)(2,1)}) conditional(s32[]{:T(128)} %convert_element_type.218, () %tuple.106, (f32[2,16,2048]{2,1,0:T(8,128)S(1)}, bf16[2048,2048]{1,0:T(8,128)(2,1)}, s32[16]{0:T(128)S(1)}, bf16[16,128,128]{2,1,0:T(8,128)(2,1)S(1)}, f32[1,16]{1,0:T(1,128)S(1)}, /*index=5*/f32[16,16]{0,1:T(8,128)S(1)}, ...), branch_computations={%region_3.4_spmd, %region_4.5_spmd} | conditional | flops 1311639808 | bytes 58082984 | solution.py:148
  854.8 4.9 convolution_add_fusion.11
  862.8 4.9 convolution_add_fusion.10
  870.8 4.9 convolution_add_fusion.9
  878.8 4.9 convolution_add_fusion.8
  885.5 1.3 collective-permute-start
  886.8 4.0 collective-permute-start.1
  890.8 2.2 collective-permute-done.1
  895.6 1.3 collective-permute-start
  896.9 36.4 %collective-permute-start.1 = (bf16[2,16,2048]{2,1,0:T(8,128)(2,1)}, bf16[2,16,2048]{2,1,0:T(8,128)(2,1)S(1)}, u32[]{:S(2)}, u32[]{:S(2)}) collective-permute-start(bf16[2,16,2048]{2,1,0:T(8,128)(2,1)} %get-tuple-element.768), channel_id=1, source_target_pairs={{32,0},{64,32},{96,64},{128,96},{160,128},{192,160},{224,192},{256... | collective-permute-start | bytes 393224 | tf_op jit(solution)/shard_map/while/body/eval_jaxpr/ppermute | solution.py:12
  933.4 2.2 collective-permute-done.1
  938.2 1.3 collective-permute-start
  939.5 4.3 collective-permute-start.1
  943.9 3.2 collective-permute-done.1
  949.6 1.3 collective-permute-start
  950.9 35.1 %collective-permute-start.1 = (bf16[2,16,2048]{2,1,0:T(8,128)(2,1)}, bf16[2,16,2048]{2,1,0:T(8,128)(2,1)S(1)}, u32[]{:S(2)}, u32[]{:S(2)}) collective-permute-start(bf16[2,16,2048]{2,1,0:T(8,128)(2,1)} %get-tuple-element.768), channel_id=1, source_target_pairs={{32,0},{64,32},{96,64},{128,96},{160,128},{192,160},{224,192},{256... | collective-permute-start | bytes 393224 | tf_op jit(solution)/shard_map/while/body/eval_jaxpr/ppermute | solution.py:12
  986.1 2.2 collective-permute-done.1
  990.9 1.3 collective-permute-start
  992.2 4.6 collective-permute-start.1
  996.9 2.2 collective-permute-done.1
  1001.7 1.3 collective-permute-start
  1003.0 35.8 %collective-permute-start.1 = (bf16[2,16,2048]{2,1,0:T(8,128)(2,1)}, bf16[2,16,2048]{2,1,0:T(8,128)(2,1)S(1)}, u32[]{:S(2)}, u32[]{:S(2)}) collective-permute-start(bf16[2,16,2048]{2,1,0:T(8,128)(2,1)} %get-tuple-element.768), channel_id=1, source_target_pairs={{32,0},{64,32},{96,64},{128,96},{160,128},{192,160},{224,192},{256... | collective-permute-start | bytes 393224 | tf_op jit(solution)/shard_map/while/body/eval_jaxpr/ppermute | solution.py:12
  1038.9 2.2 collective-permute-done.1
  1043.6 1.3 collective-permute-start
  1044.9 6.8 collective-permute-start.1
  1051.8 2.2 collective-permute-done.1
  1056.6 1.3 collective-permute-start
  1057.9 37.8 %collective-permute-start.1 = (bf16[2,16,2048]{2,1,0:T(8,128)(2,1)}, bf16[2,16,2048]{2,1,0:T(8,128)(2,1)S(1)}, u32[]{:S(2)}, u32[]{:S(2)}) collective-permute-start(bf16[2,16,2048]{2,1,0:T(8,128)(2,1)} %get-tuple-element.768), channel_id=1, source_target_pairs={{32,0},{64,32},{96,64},{128,96},{160,128},{192,160},{224,192},{256... | collective-permute-start | bytes 393224 | tf_op jit(solution)/shard_map/while/body/eval_jaxpr/ppermute | solution.py:12
  1095.8 2.2 collective-permute-done.1
  1100.6 1.3 collective-permute-start
  1101.9 6.4 collective-permute-start.1
  1108.3 2.2 collective-permute-done.1
  1113.1 1.3 collective-permute-start
  1114.4 34.0 %collective-permute-start.1 = (bf16[2,16,2048]{2,1,0:T(8,128)(2,1)}, bf16[2,16,2048]{2,1,0:T(8,128)(2,1)S(1)}, u32[]{:S(2)}, u32[]{:S(2)}) collective-permute-start(bf16[2,16,2048]{2,1,0:T(8,128)(2,1)} %get-tuple-element.768), channel_id=1, source_target_pairs={{32,0},{64,32},{96,64},{128,96},{160,128},{192,160},{224,192},{256... | collective-permute-start | bytes 393224 | tf_op jit(solution)/shard_map/while/body/eval_jaxpr/ppermute | solution.py:12
  1148.5 2.2 collective-permute-done.1
  1153.3 1.3 collective-permute-start
  1154.6 6.4 collective-permute-start.1
  1161.1 2.2 collective-permute-done.1
  1165.9 1.3 collective-permute-start
  1167.2 34.0 %collective-permute-start.1 = (bf16[2,16,2048]{2,1,0:T(8,128)(2,1)}, bf16[2,16,2048]{2,1,0:T(8,128)(2,1)S(1)}, u32[]{:S(2)}, u32[]{:S(2)}) collective-permute-start(bf16[2,16,2048]{2,1,0:T(8,128)(2,1)} %get-tuple-element.768), channel_id=1, source_target_pairs={{32,0},{64,32},{96,64},{128,96},{160,128},{192,160},{224,192},{256... | collective-permute-start | bytes 393224 | tf_op jit(solution)/shard_map/while/body/eval_jaxpr/ppermute | solution.py:12
  1201.2 2.2 collective-permute-done.1
  1206.0 1.3 collective-permute-start
  1207.3 6.4 collective-permute-start.1
  1213.8 2.2 collective-permute-done.1
  1218.6 1.3 collective-permute-start
  1219.9 34.0 %collective-permute-start.1 = (bf16[2,16,2048]{2,1,0:T(8,128)(2,1)}, bf16[2,16,2048]{2,1,0:T(8,128)(2,1)S(1)}, u32[]{:S(2)}, u32[]{:S(2)}) collective-permute-start(bf16[2,16,2048]{2,1,0:T(8,128)(2,1)} %get-tuple-element.768), channel_id=1, source_target_pairs={{32,0},{64,32},{96,64},{128,96},{160,128},{192,160},{224,192},{256... | collective-permute-start | bytes 393224 | tf_op jit(solution)/shard_map/while/body/eval_jaxpr/ppermute | solution.py:12
  1253.9 2.2 collective-permute-done.1
  1258.7 1.3 collective-permute-start
  1260.0 237.5 %collective-permute-start.1 = (bf16[2,16,2048]{2,1,0:T(8,128)(2,1)}, bf16[2,16,2048]{2,1,0:T(8,128)(2,1)S(1)}, u32[]{:S(2)}, u32[]{:S(2)}) collective-permute-start(bf16[2,16,2048]{2,1,0:T(8,128)(2,1)} %get-tuple-element.768), channel_id=1, source_target_pairs={{32,0},{64,32},{96,64},{128,96},{160,128},{192,160},{224,192},{256... | collective-permute-start | bytes 393224 | tf_op jit(solution)/shard_map/while/body/eval_jaxpr/ppermute | solution.py:12
  1497.6 2.2 collective-permute-done.1
  1499.9 33.8 %conditional.10 = (f32[2,16,2048]{2,1,0:T(8,128)}, f32[1,2,16,2048]{3,2,1,0:T(8,128)S(1)}) conditional(s32[]{:T(128)} %convert_element_type.215, () %tuple.104, (pred[]{:T(512)}, f32[1,2,16,2048]{3,2,1,0:T(8,128)S(1)}, f32[2,16,2048]{2,1,0:T(8,128)S(1)}, bf16[2048,2048]{1,0:T(8,128)(2,1)}, s32[16]{0:T(128)S(1)}, ...), branch_computations={%region_1.1_spmd, %region_2.3_spmd} | conditional | flops 1311639808 | bytes 59262640 | solution.py:135
  1503.0 4.9 convolution_add_fusion.3
  1511.0 4.9 convolution_add_fusion.2
  1519.0 4.9 convolution_add_fusion.1
  1527.0 4.9 convolution_add_fusion
  1538.5 109.4 %psum.7 = f32[1,16]{1,0:T(1,128)} all-reduce(f32[1,16]{1,0:T(1,128)S(1)} %multiply_bitcast_fusion), channel_id=1, replica_groups=mesh['slot'=16,'row'=32] {'row'}, use_global_device_ids=true, to_apply=%region_8.10 | all-reduce | flops 16 | bytes 128 | tf_op jit(solution)/shard_map/psum | solution.py:166
  (297 shorter events, 93.7 us)
Async XLA Ops:
  7.2 821.8 %all-gather.3.cloned.1.call-start = ((), (), s32[]{:S(2)}) async-start(), calls=%async_computation | async-start | bytes 8404992 | tf_op jit(solution)/shard_map/all_gather | solution.py:89
  11.2 831.0 %copy-start = (bf16[16,128,128]{2,1,0:T(8,128)(2,1)S(1)}, bf16[16,128,128]{2,1,0:T(8,128)(2,1)}, u32[]{:S(2)}) copy-start(bf16[16,128,128]{2,1,0:T(8,128)(2,1)} %param.15) | copy-start | bytes 1572868
  11.2 831.0 %copy-start.1 = (f32[2,16,2048]{2,1,0:T(8,128)S(1)}, f32[2,16,2048]{2,1,0:T(8,128)}, u32[]{:S(2)}) copy-start(f32[2,16,2048]{2,1,0:T(8,128)} %param.18) | copy-start | bytes 786436
  11.2 831.0 %copy-start.3 = (f32[2,16,2048]{2,1,0:T(8,128)S(1)}, f32[2,16,2048]{2,1,0:T(8,128)}, u32[]{:S(2)}) copy-start(f32[2,16,2048]{2,1,0:T(8,128)} %param.19) | copy-start | bytes 786436
  11.2 831.0 %copy-start.4 = (f32[1,16]{1,0:T(1,128)S(1)}, f32[1,16]{1,0:T(1,128)}, u32[]{:S(2)}) copy-start(f32[1,16]{1,0:T(1,128)} %param.17) | copy-start | bytes 196
  842.2 695.3 %copy-start.5 = (pred[16]{0:T(512)(128)(4,1)S(1)}, pred[16]{0:T(512)(128)(4,1)}, u32[]{:S(2)}) copy-start(pred[16]{0:T(512)(128)(4,1)} %get-tuple-element.588) | copy-start | bytes 52
  842.2 695.3 %copy-start.6 = (pred[16]{0:T(512)(128)(4,1)S(1)}, pred[16]{0:T(512)(128)(4,1)}, u32[]{:S(2)}) copy-start(pred[16]{0:T(512)(128)(4,1)} %get-tuple-element.620) | copy-start | bytes 52
  843.2 7.6 collective-permute-start
  844.5 6.2 collective-permute-start.1
  885.5 7.6 collective-permute-start
  886.8 6.2 collective-permute-start.1
  895.6 40.1 %collective-permute-start = (bf16[2,16,2048]{2,1,0:T(8,128)(2,1)S(1)}, bf16[2,16,2048]{2,1,0:T(8,128)(2,1)S(1)}, u32[]{:S(2)}, u32[]{:S(2)}) collective-permute-start(bf16[2,16,2048]{2,1,0:T(8,128)(2,1)S(1)} %convert_element_type.216), channel_id=1, source_target_pairs={{0,32},{32,64},{64,96},{96,128},{128,160},{160,192},{192,224},{224... | collective-permute-start | bytes 393224 | tf_op jit(solution)/shard_map/while/body/eval_jaxpr/ppermute | solution.py:12
  896.9 38.7 %collective-permute-start.1 = (bf16[2,16,2048]{2,1,0:T(8,128)(2,1)}, bf16[2,16,2048]{2,1,0:T(8,128)(2,1)S(1)}, u32[]{:S(2)}, u32[]{:S(2)}) collective-permute-start(bf16[2,16,2048]{2,1,0:T(8,128)(2,1)} %get-tuple-element.768), channel_id=1, source_target_pairs={{32,0},{64,32},{96,64},{128,96},{160,128},{192,160},{224,192},{256... | collective-permute-start | bytes 393224 | tf_op jit(solution)/shard_map/while/body/eval_jaxpr/ppermute | solution.py:12
  938.2 8.9 collective-permute-start
  939.5 7.5 collective-permute-start.1
  949.6 38.8 %collective-permute-start = (bf16[2,16,2048]{2,1,0:T(8,128)(2,1)S(1)}, bf16[2,16,2048]{2,1,0:T(8,128)(2,1)S(1)}, u32[]{:S(2)}, u32[]{:S(2)}) collective-permute-start(bf16[2,16,2048]{2,1,0:T(8,128)(2,1)S(1)} %convert_element_type.216), channel_id=1, source_target_pairs={{0,32},{32,64},{64,96},{96,128},{128,160},{160,192},{192,224},{224... | collective-permute-start | bytes 393224 | tf_op jit(solution)/shard_map/while/body/eval_jaxpr/ppermute | solution.py:12
  950.9 37.4 %collective-permute-start.1 = (bf16[2,16,2048]{2,1,0:T(8,128)(2,1)}, bf16[2,16,2048]{2,1,0:T(8,128)(2,1)S(1)}, u32[]{:S(2)}, u32[]{:S(2)}) collective-permute-start(bf16[2,16,2048]{2,1,0:T(8,128)(2,1)} %get-tuple-element.768), channel_id=1, source_target_pairs={{32,0},{64,32},{96,64},{128,96},{160,128},{192,160},{224,192},{256... | collective-permute-start | bytes 393224 | tf_op jit(solution)/shard_map/while/body/eval_jaxpr/ppermute | solution.py:12
  990.9 8.2 collective-permute-start
  992.2 6.9 collective-permute-start.1
  1001.7 39.4 %collective-permute-start = (bf16[2,16,2048]{2,1,0:T(8,128)(2,1)S(1)}, bf16[2,16,2048]{2,1,0:T(8,128)(2,1)S(1)}, u32[]{:S(2)}, u32[]{:S(2)}) collective-permute-start(bf16[2,16,2048]{2,1,0:T(8,128)(2,1)S(1)} %convert_element_type.216), channel_id=1, source_target_pairs={{0,32},{32,64},{64,96},{96,128},{128,160},{160,192},{192,224},{224... | collective-permute-start | bytes 393224 | tf_op jit(solution)/shard_map/while/body/eval_jaxpr/ppermute | solution.py:12
  1003.0 38.1 %collective-permute-start.1 = (bf16[2,16,2048]{2,1,0:T(8,128)(2,1)}, bf16[2,16,2048]{2,1,0:T(8,128)(2,1)S(1)}, u32[]{:S(2)}, u32[]{:S(2)}) collective-permute-start(bf16[2,16,2048]{2,1,0:T(8,128)(2,1)} %get-tuple-element.768), channel_id=1, source_target_pairs={{32,0},{64,32},{96,64},{128,96},{160,128},{192,160},{224,192},{256... | collective-permute-start | bytes 393224 | tf_op jit(solution)/shard_map/while/body/eval_jaxpr/ppermute | solution.py:12
  1043.6 10.4 collective-permute-start
  1044.9 9.1 collective-permute-start.1
  1056.6 41.5 %collective-permute-start = (bf16[2,16,2048]{2,1,0:T(8,128)(2,1)S(1)}, bf16[2,16,2048]{2,1,0:T(8,128)(2,1)S(1)}, u32[]{:S(2)}, u32[]{:S(2)}) collective-permute-start(bf16[2,16,2048]{2,1,0:T(8,128)(2,1)S(1)} %convert_element_type.216), channel_id=1, source_target_pairs={{0,32},{32,64},{64,96},{96,128},{128,160},{160,192},{192,224},{224... | collective-permute-start | bytes 393224 | tf_op jit(solution)/shard_map/while/body/eval_jaxpr/ppermute | solution.py:12
  1057.9 40.1 %collective-permute-start.1 = (bf16[2,16,2048]{2,1,0:T(8,128)(2,1)}, bf16[2,16,2048]{2,1,0:T(8,128)(2,1)S(1)}, u32[]{:S(2)}, u32[]{:S(2)}) collective-permute-start(bf16[2,16,2048]{2,1,0:T(8,128)(2,1)} %get-tuple-element.768), channel_id=1, source_target_pairs={{32,0},{64,32},{96,64},{128,96},{160,128},{192,160},{224,192},{256... | collective-permute-start | bytes 393224 | tf_op jit(solution)/shard_map/while/body/eval_jaxpr/ppermute | solution.py:12
  1100.6 10.0 collective-permute-start
  1101.9 8.7 collective-permute-start.1
  1113.1 37.6 %collective-permute-start = (bf16[2,16,2048]{2,1,0:T(8,128)(2,1)S(1)}, bf16[2,16,2048]{2,1,0:T(8,128)(2,1)S(1)}, u32[]{:S(2)}, u32[]{:S(2)}) collective-permute-start(bf16[2,16,2048]{2,1,0:T(8,128)(2,1)S(1)} %convert_element_type.216), channel_id=1, source_target_pairs={{0,32},{32,64},{64,96},{96,128},{128,160},{160,192},{192,224},{224... | collective-permute-start | bytes 393224 | tf_op jit(solution)/shard_map/while/body/eval_jaxpr/ppermute | solution.py:12
  1114.4 36.3 %collective-permute-start.1 = (bf16[2,16,2048]{2,1,0:T(8,128)(2,1)}, bf16[2,16,2048]{2,1,0:T(8,128)(2,1)S(1)}, u32[]{:S(2)}, u32[]{:S(2)}) collective-permute-start(bf16[2,16,2048]{2,1,0:T(8,128)(2,1)} %get-tuple-element.768), channel_id=1, source_target_pairs={{32,0},{64,32},{96,64},{128,96},{160,128},{192,160},{224,192},{256... | collective-permute-start | bytes 393224 | tf_op jit(solution)/shard_map/while/body/eval_jaxpr/ppermute | solution.py:12
  1153.3 10.0 collective-permute-start
  1154.6 8.7 collective-permute-start.1
  1165.9 37.6 %collective-permute-start = (bf16[2,16,2048]{2,1,0:T(8,128)(2,1)S(1)}, bf16[2,16,2048]{2,1,0:T(8,128)(2,1)S(1)}, u32[]{:S(2)}, u32[]{:S(2)}) collective-permute-start(bf16[2,16,2048]{2,1,0:T(8,128)(2,1)S(1)} %convert_element_type.216), channel_id=1, source_target_pairs={{0,32},{32,64},{64,96},{96,128},{128,160},{160,192},{192,224},{224... | collective-permute-start | bytes 393224 | tf_op jit(solution)/shard_map/while/body/eval_jaxpr/ppermute | solution.py:12
  1167.2 36.3 %collective-permute-start.1 = (bf16[2,16,2048]{2,1,0:T(8,128)(2,1)}, bf16[2,16,2048]{2,1,0:T(8,128)(2,1)S(1)}, u32[]{:S(2)}, u32[]{:S(2)}) collective-permute-start(bf16[2,16,2048]{2,1,0:T(8,128)(2,1)} %get-tuple-element.768), channel_id=1, source_target_pairs={{32,0},{64,32},{96,64},{128,96},{160,128},{192,160},{224,192},{256... | collective-permute-start | bytes 393224 | tf_op jit(solution)/shard_map/while/body/eval_jaxpr/ppermute | solution.py:12
  1206.0 10.0 collective-permute-start
  1207.3 8.7 collective-permute-start.1
  1218.6 37.6 %collective-permute-start = (bf16[2,16,2048]{2,1,0:T(8,128)(2,1)S(1)}, bf16[2,16,2048]{2,1,0:T(8,128)(2,1)S(1)}, u32[]{:S(2)}, u32[]{:S(2)}) collective-permute-start(bf16[2,16,2048]{2,1,0:T(8,128)(2,1)S(1)} %convert_element_type.216), channel_id=1, source_target_pairs={{0,32},{32,64},{64,96},{96,128},{128,160},{160,192},{192,224},{224... | collective-permute-start | bytes 393224 | tf_op jit(solution)/shard_map/while/body/eval_jaxpr/ppermute | solution.py:12
  1219.9 36.3 %collective-permute-start.1 = (bf16[2,16,2048]{2,1,0:T(8,128)(2,1)}, bf16[2,16,2048]{2,1,0:T(8,128)(2,1)S(1)}, u32[]{:S(2)}, u32[]{:S(2)}) collective-permute-start(bf16[2,16,2048]{2,1,0:T(8,128)(2,1)} %get-tuple-element.768), channel_id=1, source_target_pairs={{32,0},{64,32},{96,64},{128,96},{160,128},{192,160},{224,192},{256... | collective-permute-start | bytes 393224 | tf_op jit(solution)/shard_map/while/body/eval_jaxpr/ppermute | solution.py:12
  1258.7 241.1 %collective-permute-start = (bf16[2,16,2048]{2,1,0:T(8,128)(2,1)S(1)}, bf16[2,16,2048]{2,1,0:T(8,128)(2,1)S(1)}, u32[]{:S(2)}, u32[]{:S(2)}) collective-permute-start(bf16[2,16,2048]{2,1,0:T(8,128)(2,1)S(1)} %convert_element_type.216), channel_id=1, source_target_pairs={{0,32},{32,64},{64,96},{96,128},{128,160},{160,192},{192,224},{224... | collective-permute-start | bytes 393224 | tf_op jit(solution)/shard_map/while/body/eval_jaxpr/ppermute | solution.py:12
  1260.0 239.7 %collective-permute-start.1 = (bf16[2,16,2048]{2,1,0:T(8,128)(2,1)}, bf16[2,16,2048]{2,1,0:T(8,128)(2,1)S(1)}, u32[]{:S(2)}, u32[]{:S(2)}) collective-permute-start(bf16[2,16,2048]{2,1,0:T(8,128)(2,1)} %get-tuple-element.768), channel_id=1, source_target_pairs={{32,0},{64,32},{96,64},{128,96},{160,128},{192,160},{224,192},{256... | collective-permute-start | bytes 393224 | tf_op jit(solution)/shard_map/while/body/eval_jaxpr/ppermute | solution.py:12
  1534.5 113.4 %copy-start.2 = (f32[1,2,16,2048]{3,2,1,0:T(8,128)}, f32[1,2,16,2048]{3,2,1,0:T(8,128)S(1)}, u32[]{:S(2)}) copy-start(f32[1,2,16,2048]{3,2,1,0:T(8,128)S(1)} %get-tuple-element.394) | copy-start | bytes 786436
Sparse Core Ops, SparseCore 0:
  10.2 818.6 all-gather.2
where the time goes:
time: 1660 us; the launch traced here: 1650 us
  waiting for transfers between devices  855 us (52%)
  starting transfers between devices  548 us (33%)
  blocking collectives  109 us (7%)
  matrix products  54.5 us (3%)
  local copies, waits for them, and re-layouts  48.5 us (3%)
  other arithmetic  22.7 us (1%)
    all_gather x1, waiting for transfers between devices, shards(): drift_full = lax.all_gather(drift, ('slot', 'row'), axis=0, tiled=True)  818 us
    ppermute x32, starting transfers between devices, passed_along(): lax.ppermute(value, axis, [(source, source + steps) for source in range(i...  548 us
    psum x1, blocking collectives, shards(): grads = lax.psum(partial_grads[None, :], 'row')  109 us
    dot_general x8, matrix products, apply_hamiltonian(): jnp.dot(flat_rows, drift_full, preferred_element_type=jnp.float32)  39.5 us
    ppermute x32, waiting for transfers between devices, passed_along(): lax.ppermute(value, axis, [(source, source + steps) for source in range(i...  36.2 us
  transfers between devices with their start and end apart: 33, of which 17 were waited for; matrix products, arithmetic and copies ran while one was open for 0% of the time, Pallas kernels for 0%

commit v1 on v0

--- a/solution.py
+++ b/solution.py
@@ -86,7 +86,10 @@
 
 
 def shards(drift, ctrl_blocks, blk_pos, amps, init_states, targets):
-    drift_full = lax.all_gather(drift, ("slot", "row"), axis=0, tiled=True)
+    drift_full = jnp.concatenate(
+        lax.all_to_all(jnp.stack([drift] * lax.axis_size(("slot", "row"))), ("slot", "row"), 0, 0),
+        axis=0,
+    )
     block_count = drift_full.shape[0] // ctrl_blocks.shape[1]
     row_pick = blk_pos[:, 0]
     col_pick = blk_pos[:, 1]

time: 1660 us -> 1340 us (0.81)
  waiting for transfers between devices: 855 us -> 645 us
  starting transfers between devices: 548 us -> 423 us
    all_gather x1 -> x0, waiting for transfers between devices: 818 us -> none  [shards(): drift_full = lax.all_gather(drift, ('slot', 'row'), axis=0, tiled=True)]
    all_to_all x0 -> x1, waiting for transfers between devices: none -> 359 us  [shards(): lax.all_to_all(jnp.stack([drift] * lax.axis_size(('slot', 'row'))), ('slo...]
    ppermute x32, waiting for transfers between devices: 36.2 us -> 286 us  [passed_along(): lax.ppermute(value, axis, [(source, source + steps) for source in range(i...]
    ppermute x32, starting transfers between devices: 548 us -> 398 us  [passed_along(): lax.ppermute(value, axis, [(source, source + steps) for source in range(i...]
    all_to_all x0 -> x1, starting transfers between devices: none -> 25 us  [shards(): lax.all_to_all(jnp.stack([drift] * lax.axis_size(('slot', 'row'))), ('slo...]
  transfers between devices with their start and end apart: 33 -> 33, of which waited for: 17 -> 17; matrix products, arithmetic and copies ran while one was open for 0% -> 2% of each run, Pallas kernels for 0% -> 0%
where the time goes in v1:
time: 1340 us
  waiting for transfers between devices  645 us (48%)
  starting transfers between devices  423 us (32%)
  blocking collectives  110 us (8%)
  matrix products  65 us (5%)
  local copies, waits for them, and re-layouts  56.5 us (4%)
  other arithmetic  34.9 us (3%)
    ppermute x32, starting transfers between devices, passed_along(): lax.ppermute(value, axis, [(source, source + steps) for source in range(i...  398 us
    all_to_all x1, waiting for transfers between devices, shards(): lax.all_to_all(jnp.stack([drift] * lax.axis_size(('slot', 'row'))), ('slo...  359 us
    ppermute x32, waiting for transfers between devices, passed_along(): lax.ppermute(value, axis, [(source, source + steps) for source in range(i...  286 us
    psum x1, blocking collectives, shards(): grads = lax.psum(partial_grads[None, :], 'row')  110 us
    dot_general x8, matrix products, apply_hamiltonian(): jnp.dot(flat_rows, drift_full, preferred_element_type=jnp.float32)  39.5 us
  transfers between devices with their start and end apart: 33, of which 17 were waited for; matrix products, arithmetic and copies ran while one was open for 2% of the time, Pallas kernels for 0%

profile of v1, /device:TPU:103, one launch (start us, length us, event | category | flops | bytes accessed | tf_op | source)
XLA Modules:
  0.0 1338.0 jit_solution(14209233948235574569)
XLA Ops:
  0.6 8.3 stack.20
  8.9 25.0 %all-to-all-start = ((bf16[512,4,2048]{2,1,0:T(4,128)(2,1)}), bf16[512,4,2048]{2,1,0:T(4,128)(2,1)}, u32[]{:S(2)}, u32[]{:S(2)}) async-start(bf16[512,4,2048]{2,1,0:T(4,128)(2,1)} %stack.20), calls=%async_computation | async-start | bytes 16777216 | tf_op jit(solution)/shard_map/all_to_all | solution.py:90
  36.3 359.3 %all-to-all-done = bf16[512,4,2048]{2,1,0:T(4,128)(2,1)} async-done(((bf16[512,4,2048]{2,1,0:T(4,128)(2,1)}), bf16[512,4,2048]{2,1,0:T(4,128)(2,1)}, u32[]{:S(2)}, u32[]{:S(2)}) %all-to-all-start) | async-done | bytes 8388640 | tf_op jit(solution)/shard_map/all_to_all | solution.py:90
  395.6 12.5 reshape.205
  408.9 814.6 %while.23 = (s32[]{:T(128)}, f32[1,2,16,2048]{3,2,1,0:T(8,128)S(1)}, f32[2,16,2048]{2,1,0:T(8,128)}, bf16[1,2,16,2048]{3,2,1,0:T(8,128)(2,1)S(1)}, bf16[2,16,204...) while((s32[]{:T(128)}, ...), condition=%wide.region_5.7_spmd.clone.clone.clone, body=%wide.region_0.6_spmd.clone.clone.clone.sunk | while | flops 2623804928 | bytes 120887232 | solution.py:162
  409.1 2.2 collective-permute-start.1
  412.3 1.3 collective-permute-start
  414.3 4.8 collective-permute-done
  420.0 39.3 %conditional.11 = (bf16[2,16,2048]{2,1,0:T(8,128)(2,1)}) conditional(s32[]{:T(128)} %convert_element_type.218, () %tuple.106, (f32[2,16,2048]{2,1,0:T(8,128)S(1)}, bf16[2048,2048]{1,0:T(8,128)(2,1)}, s32[16]{0:T(128)}, bf16[16,128,128]{2,1,0:T(8,128)(2,1)S(1)}, f32[1,16]{1,0:T(1,128)}, /*index=5*/f32[16,16]{0,1:T(8,128)S(1)}, s32[16]{0:T(128)}, ...), branch_computations={%region_3.4_spmd, %region_4.5_spmd} | conditional | flops 1311639808 | bytes 58082984 | solution.py:151
  425.6 4.9 convolution_add_fusion.11
  434.9 4.9 convolution_add_fusion.10
  444.2 4.9 convolution_add_fusion.9
  453.6 4.9 convolution_add_fusion.8
  459.3 1.3 collective-permute-start.1
  461.5 1.3 collective-permute-start
  463.6 3.7 collective-permute-done
  468.8 40.1 %collective-permute-start.1 = (bf16[2,16,2048]{2,1,0:T(8,128)(2,1)}, bf16[2,16,2048]{2,1,0:T(8,128)(2,1)S(1)}, u32[]{:S(2)}, u32[]{:S(2)}) collective-permute-start(bf16[2,16,2048]{2,1,0:T(8,128)(2,1)} %get-tuple-element.768), channel_id=1, source_target_pairs={{32,0},{64,32},{96,64},{128,96},{160,128},{192,160},{224,192},{256... | collective-permute-start | bytes 393224 | tf_op jit(solution)/shard_map/while/body/eval_jaxpr/ppermute | solution.py:12
  509.9 1.3 collective-permute-start
  511.9 3.7 collective-permute-done
  517.1 1.9 collective-permute-start.1
  520.0 1.3 collective-permute-start
  522.1 40.4 %collective-permute-done = bf16[2,16,2048]{2,1,0:T(8,128)(2,1)S(1)} collective-permute-done((bf16[2,16,2048]{2,1,0:T(8,128)(2,1)S(1)}, bf16[2,16,2048]{2,1,0:T(8,128)(2,1)S(1)}, u32[]{:S(2)}, u32[]{:S(2)}) %collective-permute-start) | collective-permute-done | bytes 131104 | tf_op jit(solution)/shard_map/while/body/eval_jaxpr/ppermute | solution.py:12
  564.1 3.4 collective-permute-start.1
  568.4 1.3 collective-permute-start
  570.4 3.7 collective-permute-done
  575.6 38.7 %collective-permute-start.1 = (bf16[2,16,2048]{2,1,0:T(8,128)(2,1)}, bf16[2,16,2048]{2,1,0:T(8,128)(2,1)S(1)}, u32[]{:S(2)}, u32[]{:S(2)}) collective-permute-start(bf16[2,16,2048]{2,1,0:T(8,128)(2,1)} %get-tuple-element.768), channel_id=1, source_target_pairs={{32,0},{64,32},{96,64},{128,96},{160,128},{192,160},{224,192},{256... | collective-permute-start | bytes 393224 | tf_op jit(solution)/shard_map/while/body/eval_jaxpr/ppermute | solution.py:12
  615.3 1.3 collective-permute-start
  617.4 3.7 collective-permute-done
  622.6 4.0 collective-permute-start.1
  627.6 1.3 collective-permute-start
  629.6 40.4 %collective-permute-done = bf16[2,16,2048]{2,1,0:T(8,128)(2,1)S(1)} collective-permute-done((bf16[2,16,2048]{2,1,0:T(8,128)(2,1)S(1)}, bf16[2,16,2048]{2,1,0:T(8,128)(2,1)S(1)}, u32[]{:S(2)}, u32[]{:S(2)}) %collective-permute-start) | collective-permute-done | bytes 131104 | tf_op jit(solution)/shard_map/while/body/eval_jaxpr/ppermute | solution.py:12
  671.6 5.5 collective-permute-start.1
  678.0 1.3 collective-permute-start
  680.1 3.7 collective-permute-done
  685.3 36.6 %collective-permute-start.1 = (bf16[2,16,2048]{2,1,0:T(8,128)(2,1)}, bf16[2,16,2048]{2,1,0:T(8,128)(2,1)S(1)}, u32[]{:S(2)}, u32[]{:S(2)}) collective-permute-start(bf16[2,16,2048]{2,1,0:T(8,128)(2,1)} %get-tuple-element.768), channel_id=1, source_target_pairs={{32,0},{64,32},{96,64},{128,96},{160,128},{192,160},{224,192},{256... | collective-permute-start | bytes 393224 | tf_op jit(solution)/shard_map/while/body/eval_jaxpr/ppermute | solution.py:12
  722.8 1.3 collective-permute-start
  724.9 3.7 collective-permute-done
  730.1 5.5 collective-permute-start.1
  736.5 1.3 collective-permute-start
  738.6 36.9 %collective-permute-done = bf16[2,16,2048]{2,1,0:T(8,128)(2,1)S(1)} collective-permute-done((bf16[2,16,2048]{2,1,0:T(8,128)(2,1)S(1)}, bf16[2,16,2048]{2,1,0:T(8,128)(2,1)S(1)}, u32[]{:S(2)}, u32[]{:S(2)}) %collective-permute-start) | collective-permute-done | bytes 131104 | tf_op jit(solution)/shard_map/while/body/eval_jaxpr/ppermute | solution.py:12
  777.0 5.5 collective-permute-start.1
  783.4 1.3 collective-permute-start
  785.5 3.7 collective-permute-done
  790.7 56.9 %collective-permute-start.1 = (bf16[2,16,2048]{2,1,0:T(8,128)(2,1)}, bf16[2,16,2048]{2,1,0:T(8,128)(2,1)S(1)}, u32[]{:S(2)}, u32[]{:S(2)}) collective-permute-start(bf16[2,16,2048]{2,1,0:T(8,128)(2,1)} %get-tuple-element.768), channel_id=1, source_target_pairs={{32,0},{64,32},{96,64},{128,96},{160,128},{192,160},{224,192},{256... | collective-permute-start | bytes 393224 | tf_op jit(solution)/shard_map/while/body/eval_jaxpr/ppermute | solution.py:12
  848.5 1.3 collective-permute-start
  850.6 4.6 collective-permute-done
  856.7 45.0 %collective-permute-start.1 = (bf16[2,16,2048]{2,1,0:T(8,128)(2,1)}, bf16[2,16,2048]{2,1,0:T(8,128)(2,1)S(1)}, u32[]{:S(2)}, u32[]{:S(2)}) collective-permute-start(bf16[2,16,2048]{2,1,0:T(8,128)(2,1)} %get-tuple-element.768), channel_id=1, source_target_pairs={{32,0},{64,32},{96,64},{128,96},{160,128},{192,160},{224,192},{256... | collective-permute-start | bytes 393224 | tf_op jit(solution)/shard_map/while/body/eval_jaxpr/ppermute | solution.py:12
  902.7 1.3 collective-permute-start
  904.7 43.2 %collective-permute-done = bf16[2,16,2048]{2,1,0:T(8,128)(2,1)S(1)} collective-permute-done((bf16[2,16,2048]{2,1,0:T(8,128)(2,1)S(1)}, bf16[2,16,2048]{2,1,0:T(8,128)(2,1)S(1)}, u32[]{:S(2)}, u32[]{:S(2)}) %collective-permute-start) | collective-permute-done | bytes 131104 | tf_op jit(solution)/shard_map/while/body/eval_jaxpr/ppermute | solution.py:12
  949.4 42.9 %collective-permute-start.1 = (bf16[2,16,2048]{2,1,0:T(8,128)(2,1)}, bf16[2,16,2048]{2,1,0:T(8,128)(2,1)S(1)}, u32[]{:S(2)}, u32[]{:S(2)}) collective-permute-start(bf16[2,16,2048]{2,1,0:T(8,128)(2,1)} %get-tuple-element.768), channel_id=1, source_target_pairs={{32,0},{64,32},{96,64},{128,96},{160,128},{192,160},{224,192},{256... | collective-permute-start | bytes 393224 | tf_op jit(solution)/shard_map/while/body/eval_jaxpr/ppermute | solution.py:12
  993.3 1.3 collective-permute-start
  995.4 43.2 %collective-permute-done = bf16[2,16,2048]{2,1,0:T(8,128)(2,1)S(1)} collective-permute-done((bf16[2,16,2048]{2,1,0:T(8,128)(2,1)S(1)}, bf16[2,16,2048]{2,1,0:T(8,128)(2,1)S(1)}, u32[]{:S(2)}, u32[]{:S(2)}) %collective-permute-start) | collective-permute-done | bytes 131104 | tf_op jit(solution)/shard_map/while/body/eval_jaxpr/ppermute | solution.py:12
  1040.1 45.0 %collective-permute-start.1 = (bf16[2,16,2048]{2,1,0:T(8,128)(2,1)}, bf16[2,16,2048]{2,1,0:T(8,128)(2,1)S(1)}, u32[]{:S(2)}, u32[]{:S(2)}) collective-permute-start(bf16[2,16,2048]{2,1,0:T(8,128)(2,1)} %get-tuple-element.768), channel_id=1, source_target_pairs={{32,0},{64,32},{96,64},{128,96},{160,128},{192,160},{224,192},{256... | collective-permute-start | bytes 393224 | tf_op jit(solution)/shard_map/while/body/eval_jaxpr/ppermute | solution.py:12
  1086.1 1.3 collective-permute-start
  1088.1 43.2 %collective-permute-done = bf16[2,16,2048]{2,1,0:T(8,128)(2,1)S(1)} collective-permute-done((bf16[2,16,2048]{2,1,0:T(8,128)(2,1)S(1)}, bf16[2,16,2048]{2,1,0:T(8,128)(2,1)S(1)}, u32[]{:S(2)}, u32[]{:S(2)}) %collective-permute-start) | collective-permute-done | bytes 131104 | tf_op jit(solution)/shard_map/while/body/eval_jaxpr/ppermute | solution.py:12
  1132.9 42.9 %collective-permute-start.1 = (bf16[2,16,2048]{2,1,0:T(8,128)(2,1)}, bf16[2,16,2048]{2,1,0:T(8,128)(2,1)S(1)}, u32[]{:S(2)}, u32[]{:S(2)}) collective-permute-start(bf16[2,16,2048]{2,1,0:T(8,128)(2,1)} %get-tuple-element.768), channel_id=1, source_target_pairs={{32,0},{64,32},{96,64},{128,96},{160,128},{192,160},{224,192},{256... | collective-permute-start | bytes 393224 | tf_op jit(solution)/shard_map/while/body/eval_jaxpr/ppermute | solution.py:12
  1176.7 1.3 collective-permute-start
  1178.8 3.7 collective-permute-done
  1182.5 40.3 %conditional.10 = (f32[2,16,2048]{2,1,0:T(8,128)}, f32[1,2,16,2048]{3,2,1,0:T(8,128)S(1)}) conditional(s32[]{:T(128)} %convert_element_type.215, () %tuple.104, (pred[]{:T(512)}, f32[1,2,16,2048]{3,2,1,0:T(8,128)S(1)}, f32[2,16,2048]{2,1,0:T(8,128)S(1)}, bf16[2048,2048]{1,0:T(8,128)(2,1)}, s32[16]{0:T(128)}, ...), branch_computations={%region_1.1_spmd, %region_2.3_spmd} | conditional | flops 1311639808 | bytes 59262640 | solution.py:138
  1188.1 4.9 convolution_add_fusion.3
  1197.4 4.9 convolution_add_fusion.2
  1206.7 4.9 convolution_add_fusion.1
  1216.1 4.9 convolution_add_fusion
  1227.5 110.5 %psum.7 = f32[1,16]{1,0:T(1,128)} all-reduce(f32[1,16]{1,0:T(1,128)S(1)} %multiply_bitcast_fusion), channel_id=1, replica_groups=mesh['slot'=16,'row'=32] {'row'}, use_global_device_ids=true, to_apply=%region_8.10 | all-reduce | flops 16 | bytes 128 | tf_op jit(solution)/shard_map/psum | solution.py:169
  (297 shorter events, 117.4 us)
Async XLA Ops:
  8.9 25.1 %copy-start.4 = (s32[16,2]{0,1:T(2,128)S(1)}, s32[16,2]{0,1:T(2,128)}, u32[]{:S(2)}) copy-start(s32[16,2]{0,1:T(2,128)} %param.16) | copy-start | bytes 388
  8.9 386.7 %all-to-all-start = ((bf16[512,4,2048]{2,1,0:T(4,128)(2,1)}), bf16[512,4,2048]{2,1,0:T(4,128)(2,1)}, u32[]{:S(2)}, u32[]{:S(2)}) async-start(bf16[512,4,2048]{2,1,0:T(4,128)(2,1)} %stack.20), calls=%async_computation | async-start | bytes 16777216 | tf_op jit(solution)/shard_map/all_to_all | solution.py:90
  36.3 372.5 %copy-start = (bf16[16,128,128]{2,1,0:T(8,128)(2,1)S(1)}, bf16[16,128,128]{2,1,0:T(8,128)(2,1)}, u32[]{:S(2)}) copy-start(bf16[16,128,128]{2,1,0:T(8,128)(2,1)} %param.15) | copy-start | bytes 1572868
  36.3 372.5 %copy-start.1 = (f32[2,16,2048]{2,1,0:T(8,128)S(1)}, f32[2,16,2048]{2,1,0:T(8,128)}, u32[]{:S(2)}) copy-start(f32[2,16,2048]{2,1,0:T(8,128)} %param.18) | copy-start | bytes 786436
  36.3 372.5 %copy-start.3 = (f32[2,16,2048]{2,1,0:T(8,128)S(1)}, f32[2,16,2048]{2,1,0:T(8,128)}, u32[]{:S(2)}) copy-start(f32[2,16,2048]{2,1,0:T(8,128)} %param.19) | copy-start | bytes 786436
  408.9 817.7 %copy-start.5 = (pred[16]{0:T(512)(128)(4,1)S(1)}, pred[16]{0:T(512)(128)(4,1)}, u32[]{:S(2)}) copy-start(pred[16]{0:T(512)(128)(4,1)} %get-tuple-element.588) | copy-start | bytes 52
  408.9 817.7 %copy-start.6 = (pred[16]{0:T(512)(128)(4,1)S(1)}, pred[16]{0:T(512)(128)(4,1)}, u32[]{:S(2)}) copy-start(pred[16]{0:T(512)(128)(4,1)} %get-tuple-element.620) | copy-start | bytes 52
  409.1 5.2 collective-permute-start.1
  412.3 6.8 collective-permute-start
  459.3 4.2 collective-permute-start.1
  461.5 5.7 collective-permute-start
  468.8 43.1 %collective-permute-start.1 = (bf16[2,16,2048]{2,1,0:T(8,128)(2,1)}, bf16[2,16,2048]{2,1,0:T(8,128)(2,1)S(1)}, u32[]{:S(2)}, u32[]{:S(2)}) collective-permute-start(bf16[2,16,2048]{2,1,0:T(8,128)(2,1)} %get-tuple-element.768), channel_id=1, source_target_pairs={{32,0},{64,32},{96,64},{128,96},{160,128},{192,160},{224,192},{256... | collective-permute-start | bytes 393224 | tf_op jit(solution)/shard_map/while/body/eval_jaxpr/ppermute | solution.py:12
  509.9 5.7 collective-permute-start
  517.1 4.9 collective-permute-start.1
  520.0 42.5 %collective-permute-start = (bf16[2,16,2048]{2,1,0:T(8,128)(2,1)S(1)}, bf16[2,16,2048]{2,1,0:T(8,128)(2,1)S(1)}, u32[]{:S(2)}, u32[]{:S(2)}) collective-permute-start(bf16[2,16,2048]{2,1,0:T(8,128)(2,1)S(1)} %convert_element_type.216), channel_id=1, source_target_pairs={{0,32},{32,64},{64,96},{96,128},{128,160},{160,192},{192,224},{224... | collective-permute-start | bytes 393224 | tf_op jit(solution)/shard_map/while/body/eval_jaxpr/ppermute | solution.py:12
  564.1 6.3 collective-permute-start.1
  568.4 5.7 collective-permute-start
  575.6 41.6 %collective-permute-start.1 = (bf16[2,16,2048]{2,1,0:T(8,128)(2,1)}, bf16[2,16,2048]{2,1,0:T(8,128)(2,1)S(1)}, u32[]{:S(2)}, u32[]{:S(2)}) collective-permute-start(bf16[2,16,2048]{2,1,0:T(8,128)(2,1)} %get-tuple-element.768), channel_id=1, source_target_pairs={{32,0},{64,32},{96,64},{128,96},{160,128},{192,160},{224,192},{256... | collective-permute-start | bytes 393224 | tf_op jit(solution)/shard_map/while/body/eval_jaxpr/ppermute | solution.py:12
  615.3 5.7 collective-permute-start
  622.6 7.0 collective-permute-start.1
  627.6 42.5 %collective-permute-start = (bf16[2,16,2048]{2,1,0:T(8,128)(2,1)S(1)}, bf16[2,16,2048]{2,1,0:T(8,128)(2,1)S(1)}, u32[]{:S(2)}, u32[]{:S(2)}) collective-permute-start(bf16[2,16,2048]{2,1,0:T(8,128)(2,1)S(1)} %convert_element_type.216), channel_id=1, source_target_pairs={{0,32},{32,64},{64,96},{96,128},{128,160},{160,192},{192,224},{224... | collective-permute-start | bytes 393224 | tf_op jit(solution)/shard_map/while/body/eval_jaxpr/ppermute | solution.py:12
  671.6 8.4 collective-permute-start.1
  678.0 5.7 collective-permute-start
  685.3 39.5 %collective-permute-start.1 = (bf16[2,16,2048]{2,1,0:T(8,128)(2,1)}, bf16[2,16,2048]{2,1,0:T(8,128)(2,1)S(1)}, u32[]{:S(2)}, u32[]{:S(2)}) collective-permute-start(bf16[2,16,2048]{2,1,0:T(8,128)(2,1)} %get-tuple-element.768), channel_id=1, source_target_pairs={{32,0},{64,32},{96,64},{128,96},{160,128},{192,160},{224,192},{256... | collective-permute-start | bytes 393224 | tf_op jit(solution)/shard_map/while/body/eval_jaxpr/ppermute | solution.py:12
  722.8 5.7 collective-permute-start
  730.1 8.4 collective-permute-start.1
  736.5 38.9 %collective-permute-start = (bf16[2,16,2048]{2,1,0:T(8,128)(2,1)S(1)}, bf16[2,16,2048]{2,1,0:T(8,128)(2,1)S(1)}, u32[]{:S(2)}, u32[]{:S(2)}) collective-permute-start(bf16[2,16,2048]{2,1,0:T(8,128)(2,1)S(1)} %convert_element_type.216), channel_id=1, source_target_pairs={{0,32},{32,64},{64,96},{96,128},{128,160},{160,192},{192,224},{224... | collective-permute-start | bytes 393224 | tf_op jit(solution)/shard_map/while/body/eval_jaxpr/ppermute | solution.py:12
  777.0 8.4 collective-permute-start.1
  783.4 5.7 collective-permute-start
  790.7 59.8 %collective-permute-start.1 = (bf16[2,16,2048]{2,1,0:T(8,128)(2,1)}, bf16[2,16,2048]{2,1,0:T(8,128)(2,1)S(1)}, u32[]{:S(2)}, u32[]{:S(2)}) collective-permute-start(bf16[2,16,2048]{2,1,0:T(8,128)(2,1)} %get-tuple-element.768), channel_id=1, source_target_pairs={{32,0},{64,32},{96,64},{128,96},{160,128},{192,160},{224,192},{256... | collective-permute-start | bytes 393224 | tf_op jit(solution)/shard_map/while/body/eval_jaxpr/ppermute | solution.py:12
  848.5 6.6 collective-permute-start
  856.7 47.9 %collective-permute-start.1 = (bf16[2,16,2048]{2,1,0:T(8,128)(2,1)}, bf16[2,16,2048]{2,1,0:T(8,128)(2,1)S(1)}, u32[]{:S(2)}, u32[]{:S(2)}) collective-permute-start(bf16[2,16,2048]{2,1,0:T(8,128)(2,1)} %get-tuple-element.768), channel_id=1, source_target_pairs={{32,0},{64,32},{96,64},{128,96},{160,128},{192,160},{224,192},{256... | collective-permute-start | bytes 393224 | tf_op jit(solution)/shard_map/while/body/eval_jaxpr/ppermute | solution.py:12
  902.7 45.2 %collective-permute-start = (bf16[2,16,2048]{2,1,0:T(8,128)(2,1)S(1)}, bf16[2,16,2048]{2,1,0:T(8,128)(2,1)S(1)}, u32[]{:S(2)}, u32[]{:S(2)}) collective-permute-start(bf16[2,16,2048]{2,1,0:T(8,128)(2,1)S(1)} %convert_element_type.216), channel_id=1, source_target_pairs={{0,32},{32,64},{64,96},{96,128},{128,160},{160,192},{192,224},{224... | collective-permute-start | bytes 393224 | tf_op jit(solution)/shard_map/while/body/eval_jaxpr/ppermute | solution.py:12
  949.4 45.8 %collective-permute-start.1 = (bf16[2,16,2048]{2,1,0:T(8,128)(2,1)}, bf16[2,16,2048]{2,1,0:T(8,128)(2,1)S(1)}, u32[]{:S(2)}, u32[]{:S(2)}) collective-permute-start(bf16[2,16,2048]{2,1,0:T(8,128)(2,1)} %get-tuple-element.768), channel_id=1, source_target_pairs={{32,0},{64,32},{96,64},{128,96},{160,128},{192,160},{224,192},{256... | collective-permute-start | bytes 393224 | tf_op jit(solution)/shard_map/while/body/eval_jaxpr/ppermute | solution.py:12
  993.3 45.2 %collective-permute-start = (bf16[2,16,2048]{2,1,0:T(8,128)(2,1)S(1)}, bf16[2,16,2048]{2,1,0:T(8,128)(2,1)S(1)}, u32[]{:S(2)}, u32[]{:S(2)}) collective-permute-start(bf16[2,16,2048]{2,1,0:T(8,128)(2,1)S(1)} %convert_element_type.216), channel_id=1, source_target_pairs={{0,32},{32,64},{64,96},{96,128},{128,160},{160,192},{192,224},{224... | collective-permute-start | bytes 393224 | tf_op jit(solution)/shard_map/while/body/eval_jaxpr/ppermute | solution.py:12
  1040.1 47.9 %collective-permute-start.1 = (bf16[2,16,2048]{2,1,0:T(8,128)(2,1)}, bf16[2,16,2048]{2,1,0:T(8,128)(2,1)S(1)}, u32[]{:S(2)}, u32[]{:S(2)}) collective-permute-start(bf16[2,16,2048]{2,1,0:T(8,128)(2,1)} %get-tuple-element.768), channel_id=1, source_target_pairs={{32,0},{64,32},{96,64},{128,96},{160,128},{192,160},{224,192},{256... | collective-permute-start | bytes 393224 | tf_op jit(solution)/shard_map/while/body/eval_jaxpr/ppermute | solution.py:12
  1086.1 45.2 %collective-permute-start = (bf16[2,16,2048]{2,1,0:T(8,128)(2,1)S(1)}, bf16[2,16,2048]{2,1,0:T(8,128)(2,1)S(1)}, u32[]{:S(2)}, u32[]{:S(2)}) collective-permute-start(bf16[2,16,2048]{2,1,0:T(8,128)(2,1)S(1)} %convert_element_type.216), channel_id=1, source_target_pairs={{0,32},{32,64},{64,96},{96,128},{128,160},{160,192},{192,224},{224... | collective-permute-start | bytes 393224 | tf_op jit(solution)/shard_map/while/body/eval_jaxpr/ppermute | solution.py:12
  1132.9 45.8 %collective-permute-start.1 = (bf16[2,16,2048]{2,1,0:T(8,128)(2,1)}, bf16[2,16,2048]{2,1,0:T(8,128)(2,1)S(1)}, u32[]{:S(2)}, u32[]{:S(2)}) collective-permute-start(bf16[2,16,2048]{2,1,0:T(8,128)(2,1)} %get-tuple-element.768), channel_id=1, source_target_pairs={{32,0},{64,32},{96,64},{128,96},{160,128},{192,160},{224,192},{256... | collective-permute-start | bytes 393224 | tf_op jit(solution)/shard_map/while/body/eval_jaxpr/ppermute | solution.py:12
  1176.7 5.7 collective-permute-start
  1223.5 114.5 %copy-start.2 = (f32[1,2,16,2048]{3,2,1,0:T(8,128)}, f32[1,2,16,2048]{3,2,1,0:T(8,128)S(1)}, u32[]{:S(2)}) copy-start(f32[1,2,16,2048]{3,2,1,0:T(8,128)S(1)} %get-tuple-element.394) | copy-start | bytes 786436
